TPU v7x, 32 devices: a whole 2x2x4 slice. The times are simulated.
32 devices in a mesh: ctx: 8 (over z, core), chan: 4 (over y, x).
Axes of the slice: x: 2, y: 2, z: 4, core: 2. Of those that a mesh axis runs over, the one named last changes fastest.
Arguments:
- frames: bfloat16 [2, 9216, 1536], P(None, 'ctx'), may hold values from -6 to 6
- ln_gain: float32 [1536], replicated, may hold values from 0.5 to 1.5
- ln_bias: float32 [1536], replicated, may hold values from -3 to 3
- w_in: bfloat16 [1536, 2, 1536], P('ctx', None, 'chan'), may hold values from -0.15625 to 0.15625
- w_depth: float32 [31, 1536], P(None, 'chan'), may hold values from -1 to 1
- bn_gain: float32 [1536], P('chan'), may hold values from 0.1 to 1.9
- bn_bias: float32 [1536], P('chan'), may hold values from -3 to 3
- w_out: bfloat16 [1536, 1536], P('ctx', 'chan'), may hold values from -0.15625 to 0.15625
- lengths: int32 [2], replicated, may hold values from 2304 to 9216, as said below
- grad_out: bfloat16 [2, 9216, 1536], P(None, 'ctx'), may hold values from -6 to 6
Outputs:
- block_out: bfloat16 [2, 9216, 1536], P(None, 'ctx', 'chan')
- grad_frames: bfloat16 [2, 9216, 1536], P(None, 'ctx', 'chan')
- grad_w_in: float32 [1536, 2, 1536], P('ctx', None, 'chan')
- grad_w_out: float32 [1536, 1536], P('ctx', 'chan')
- grad_w_depth: float32 [31, 1536], P(None, 'chan')
- grad_bn: float32 [2, 1536], P(None, 'chan')
- grad_ln: float32 [2, 1536], P(None, 'chan')
Inputs may be any that keep to these rules, and one draw needn't show every extreme that they name: `lengths`: recording 0 always has all 9216 frames valid.
All inputs are finite; a program needn't handle non-finite values.
Results may differ from a plain program's by a relative error of at most 0.018.
Values may be sent and summed in bfloat16 or wider, within the bound.
A program may use at most 192 MiB of HBM per device.

v0:
```python
import jax
import jax.numpy as jnp
from jax import lax
from jax.sharding import PartitionSpec as P

epsilon = 1e-05


def padded_2(shard, sides, width):
    for axis, dim in sides:
        devices, length = (lax.axis_size(axis), shard.shape[dim])
        up = [(i, (i + 1) % devices) for i in range(devices - 1)]
        down = [(j, i) for i, j in up]
        last = lax.slice_in_dim(shard, length - width, length, axis=dim)
        initial = lax.slice_in_dim(shard, 0, width, axis=dim)
        before = lax.ppermute(last, axis, up)
        after = lax.ppermute(initial, axis, down)
        shard = jnp.concatenate([before, shard, after], axis=dim)
    return shard


def contract(left_op, right_op, left_dim, right_dim):
    return lax.dot_general(
        left_op,
        right_op,
        (((left_dim,), (right_dim,)), ((), ())),
        preferred_element_type=jnp.float32,
    )


def on_device(frames, ln_gain, ln_bias, w_in, w_depth, bn_gain, bn_bias, w_out, lengths, grad_out):
    records, local_len, model_width = frames.shape
    shard_in = w_in.shape[0]
    channels = w_in.shape[2]
    tap_count = w_depth.shape[0]
    margin = (tap_count - 1) // 2
    local_rows = records * local_len
    chan_start = lax.axis_index("chan") * channels
    position = lax.axis_index("ctx") * local_len + jnp.arange(local_len, dtype=jnp.int32)
    valid_mask = (position[None, :] < lengths[:, None]).astype(jnp.float32)[:, :, None]
    frame_count = jnp.sum(lengths.astype(jnp.float32))
    inputs = frames.astype(jnp.float32)
    centred = inputs - jnp.mean(inputs, axis=-1, keepdims=True)
    ln_rstd = lax.rsqrt(jnp.mean(centred * centred, axis=-1, keepdims=True) + epsilon)
    ln_hat = centred * ln_rstd
    normed = (ln_hat * ln_gain + ln_bias).astype(jnp.bfloat16)
    normed_rows = normed.reshape(local_rows, model_width)
    shard_piece = lax.all_gather(w_in, "ctx", axis=0, tiled=True)
    piece_rows = shard_piece.shape[0]
    projected = jnp.dot(
        normed_rows,
        shard_piece.reshape(piece_rows, 2 * channels),
        preferred_element_type=jnp.float32,
    )
    projected = projected.reshape(records, local_len, 2, channels)
    values = projected[:, :, 0]
    gate_vals = jax.nn.sigmoid(projected[:, :, 1])
    glu_out = (values * gate_vals * valid_mask).astype(jnp.bfloat16)
    padded = padded_2(glu_out, (("ctx", 1),), margin).astype(jnp.float32)
    depth_out = jnp.zeros((records, local_len, channels), jnp.float32)
    for offset in range(tap_count):
        depth_out = depth_out + padded[:, offset : offset + local_len] * w_depth[offset]
    bn_mean = lax.psum(jnp.sum(depth_out * valid_mask, axis=(0, 1)), "ctx") / frame_count
    bn_cent = (depth_out - bn_mean) * valid_mask
    bn_var = lax.psum(jnp.sum(bn_cent * bn_cent, axis=(0, 1)), "ctx") / frame_count
    bn_rstd = lax.rsqrt(bn_var + epsilon)
    bn_hat = (depth_out - bn_mean) * bn_rstd
    bn_out = bn_hat * bn_gain + bn_bias
    swish_gate = jax.nn.sigmoid(bn_out)
    activated = (bn_out * swish_gate * valid_mask).astype(jnp.bfloat16)
    act_rows = activated.reshape(local_rows, channels)
    proj_out = contract(act_rows, lax.all_gather(w_out, "ctx", axis=0, tiled=True), 1, 1)
    own_out = lax.psum_scatter(
        proj_out.astype(jnp.bfloat16), "chan", scatter_dimension=1, tiled=True
    ).astype(jnp.float32)
    input_rows = inputs.reshape(local_rows, model_width)
    own_inputs = lax.dynamic_slice_in_dim(input_rows, chan_start, channels, 1)
    block_out = (own_inputs + own_out).astype(jnp.bfloat16).reshape(records, local_len, channels)
    grad_rows = grad_out.reshape(local_rows, model_width)
    picked = grad_rows
    grad_w_out = lax.psum_scatter(
        contract(picked, act_rows, 0, 0).astype(jnp.bfloat16),
        "ctx",
        scatter_dimension=0,
        tiled=True,
    ).astype(jnp.float32)
    picked = grad_rows
    grad_act = jnp.dot(
        picked, lax.all_gather(w_out, "ctx", axis=0, tiled=True), preferred_element_type=jnp.float32
    )
    grad_act = grad_act.reshape(records, local_len, channels)
    grad_bn_out = grad_act * valid_mask * (swish_gate * (1.0 + bn_out * (1.0 - swish_gate)))
    gain_sum, bias_sum = lax.psum(
        (jnp.sum(grad_bn_out * bn_hat, axis=(0, 1)), jnp.sum(grad_bn_out, axis=(0, 1))), "ctx"
    )
    grad_depth = (
        valid_mask
        * (bn_gain * bn_rstd)
        * (grad_bn_out - (bias_sum + bn_hat * gain_sum) / frame_count)
    )
    grad_padded = padded_2(grad_depth, (("ctx", 1),), margin)
    depth_local = jnp.stack(
        [
            jnp.sum(grad_depth * padded[:, offset : offset + local_len], axis=(0, 1))
            for offset in range(tap_count)
        ]
    )
    grad_glu = jnp.zeros((records, local_len, channels), jnp.float32)
    for offset in range(tap_count):
        begin_at = tap_count - 1 - offset
        grad_glu = grad_glu + grad_padded[:, begin_at : begin_at + local_len] * w_depth[offset]
    grad_glu = grad_glu * valid_mask
    grad_values = grad_glu * gate_vals
    grad_gates = grad_glu * values * gate_vals * (1.0 - gate_vals)
    grad_proj = (
        jnp.stack([grad_values, grad_gates], axis=2)
        .astype(jnp.bfloat16)
        .reshape(local_rows, 2 * channels)
    )
    picked = normed_rows
    grad_w_in = lax.psum_scatter(
        contract(picked, grad_proj, 0, 0)
        .reshape(shard_in * lax.axis_size("ctx"), 2, channels)
        .astype(jnp.bfloat16),
        "ctx",
        scatter_dimension=0,
        tiled=True,
    ).astype(jnp.float32)
    shard_piece = lax.all_gather(w_in, "ctx", axis=0, tiled=True)
    grad_part = contract(grad_proj, shard_piece.reshape(shard_piece.shape[0], 2 * channels), 1, 1)
    hat_rows = ln_hat.reshape(local_rows, model_width)
    rstd_rows = ln_rstd.reshape(local_rows, 1)
    own_hat = lax.dynamic_slice_in_dim(hat_rows, chan_start, channels, 1)
    own_grad = lax.psum_scatter(
        grad_part.astype(jnp.bfloat16), "chan", scatter_dimension=1, tiled=True
    ).astype(jnp.float32)
    own_gain = lax.dynamic_slice_in_dim(ln_gain, chan_start, channels, 0)
    own_scaled = own_grad * own_gain
    first_rows, second_rows = lax.psum(
        (jnp.sum(own_scaled, axis=1), jnp.sum(own_scaled * own_hat, axis=1)), "chan"
    )
    own_dx = rstd_rows * (
        own_scaled
        - first_rows[:, None] / model_width
        - own_hat * (second_rows[:, None] / model_width)
    )
    own_cotangent = lax.dynamic_slice_in_dim(grad_rows, chan_start, channels, 1).astype(jnp.float32)
    grad_frames = (
        (own_dx + own_cotangent).astype(jnp.bfloat16).reshape(records, local_len, channels)
    )
    ln_local = jnp.stack([jnp.sum(own_grad * own_hat, axis=0), jnp.sum(own_grad, axis=0)])
    grad_w_depth, grad_ln = lax.psum((depth_local, ln_local), "ctx")
    grad_bn = jnp.stack([gain_sum, bias_sum])
    return (block_out, grad_frames, grad_w_in, grad_w_out, grad_w_depth, grad_bn, grad_ln)


def solution(mesh):
    in_specs = (
        P(None, "ctx", None),
        P(),
        P(),
        P("ctx", None, "chan"),
        P(None, "chan"),
        P("chan"),
        P("chan"),
        P("ctx", "chan"),
        P(),
        P(None, "ctx", None),
    )
    out_specs = (
        P(None, "ctx", "chan"),
        P(None, "ctx", "chan"),
        P("ctx", None, "chan"),
        P("ctx", "chan"),
        P(None, "chan"),
        P(None, "chan"),
        P(None, "chan"),
    )
    return jax.shard_map(
        on_device, mesh=mesh, in_specs=in_specs, out_specs=out_specs, check_vma=False
    )
```

profile of v0, /device:TPU:0, one launch (start us, length us, event | category | flops | bytes accessed | tf_op | source)
XLA Modules:
  0.0 555.2 jit_solution(12352163008588690644)
XLA Ops:
  8.7 1.9 slice_reduce_fusion.30
  10.6 1.7 slice_reduce_fusion.29
  12.2 4.2 convert_reduce_fusion
  17.3 2.0 multiply_reduce_fusion
  19.4 10.8 %subtract_multiply_fusion = (f32[2,1152,1536]{2,1,0:T(8,128)}, bf16[2,1152,1536]{2,1,0:T(8,128)(2,1)}) fusion(bf16[2,1152,1536]{2,1,0:T(8,128)(2,1)} %param.10, f32[2,1152]{1,0:T(2,128)S(1)} %add_rsqrt_fusion, f32[2,1152]{1,0:T(2,128)S(1)} %broadcast_multiply_fusion.2, f32[1536]{0:T(1024)S(1)} %copy-done.42, f32[1536]{0:T(1024)S(1)} %copy-done.41), kind=kLoop, calls=%fused_computation.30 | loop fusion | flops 21233664 | bytes 28342272 | tf_op jit(solution)/shard_map/mul | solution.py:45
  30.1 13.6 %all-gather.3.cloned.1.call-done = bf16[1536,2,384]{2,1,0:T(2,128)(2,1)} async-done(((bf16[192,2,384]{2,1,0:T(2,128)(2,1)}), bf16[1536,2,384]{2,1,0:T(2,128)(2,1)}) %all-gather.3.cloned.1.call-update) | async-done | bytes 2359312 | tf_op jit(solution)/shard_map/all_gather | solution.py:48
  43.8 2.1 copy.50
  45.9 2.8 copy.31
  48.8 8.7 %fusion = f32[2,1152,2,384]{3,1,2,0:T(8,128)S(1)} fusion(bf16[2,384,1536,1]{2,1,0,3:T(8,128)(2,1)} %bitcast.89, bf16[2,1152,1536]{2,1,0:T(8,128)(2,1)} %get-tuple-element.110), kind=kOutput, calls=%fused_computation.35 | convolution fusion | flops 5435817984 | bytes 16515072 | tf_op jit(solution)/shard_map/dot_general | solution.py:50
  58.7 1.8 copy-done.3
  61.7 2.1 collective-permute-start
  63.8 1.3 collective-permute-start.1
  65.7 1.9 collective-permute-done.1
  67.5 8.8 %concatenate.38 = bf16[2,1182,384]{2,1,0:T(8,128)(2,1)S(1)} concatenate(bf16[2,15,384]{2,1,0:T(8,128)(2,1)S(1)} %collective-permute-done, bf16[2,1152,384]{2,1,0:T(8,128)(2,1)} %copy-done.6, bf16[2,15,384]{2,1,0:T(8,128)(2,1)S(1)} %collective-permute-done.1), dimensions={1} | concatenate | bytes 3631104 | tf_op jit(solution)/shard_map/concatenate | solution.py:18
  77.3 15.3 %multiply_reduce_fusion.34 = (f32[384]{0:T(512)}, f32[2,1152,384]{2,1,0:T(8,128)S(1)}) fusion(f32[2,1152]{1,0:T(2,128)S(1)} %compare_convert_fusion, f32[384]{0:T(512)S(1)} %copy-done.39, f32[2,1182,384]{2,1,0:T(8,128)S(1)} %convert_element_type.79, f32[384]{0:T(512)S(1)} %copy-done.40, f32[384]{0:T(512)S(1)} %copy-done.10, f32[384]{0:T(512)S(1)} %copy-done.11, ...), kind=kLoop, calls=%fused_computation.209 | loop fusion | flops 55737984 | bytes 113304576 | tf_op jit(solution)/shard_map/reduce_sum | solution.py:63
  92.6 16.8 %psum.56 = f32[384]{0:T(512)} all-reduce(f32[384]{0:T(512)} %get-tuple-element.107), channel_id=1, replica_groups=mesh['ctx'=8,'chan'=4] {'ctx'}, use_global_device_ids=true, to_apply=%region_3.0 | all-reduce | flops 384 | bytes 3072 | tf_op jit(solution)/shard_map/psum | solution.py:63
  109.4 1.3 broadcast_divide_fusion
  112.4 14.7 %psum.57 = f32[384]{0:T(512)} all-reduce(f32[384]{0:T(512)} %multiply_reduce_fusion.33), channel_id=1, replica_groups=mesh['ctx'=8,'chan'=4] {'ctx'}, use_global_device_ids=true, to_apply=%region_6.0 | all-reduce | flops 384 | bytes 3072 | tf_op jit(solution)/shard_map/psum | solution.py:65
  127.2 1.9 fusion.110
  129.1 10.3 %fusion.108 = (f32[384]{0:T(512)}, f32[384]{0:T(512)}, bf16[2,1152,384]{2,1,0:T(8,128)(2,1)}, f32[2,1152,384]{2,1,0:T(8,128)}) fusion(f32[384]{0:T(512)} %get-tuple-element.106, f32[2,1152,384]{2,1,0:T(8,128)S(1)} %get-tuple-element.108, f32[384]{0:T(512)} %copy-done.28, f32[2,1152]{1,0:T(2,128)S(1)} %compare_convert_fusion, f32[384]{0:T(512)} %param.16, ...), kind=kOutput, calls=%fused_computation.260 | convolution fusion | flops 2734717952 | bytes 17123328 | tf_op jit(solution)/shard_map/dot_general | solution.py:88
  139.4 14.3 %all-reduce.1 = (f32[384]{0:T(512)}, f32[384]{0:T(512)}) all-reduce(f32[384]{0:T(512)} %get-tuple-element.62, f32[384]{0:T(512)} %get-tuple-element.61), channel_id=1, replica_groups=mesh['ctx'=8,'chan'=4] {'ctx'}, use_global_device_ids=true, to_apply=%region_11.0 | all-reduce | flops 768 | bytes 6144 | tf_op jit(solution)/shard_map/psum | solution.py:93
  153.7 40.0 %multiply_reduce_fusion.1 = (f32[384]{0:T(512)}, f32[384]{0:T(512)}, f32[384]{0:T(512)}, f32[384]{0:T(512)}, f32[384]{0:T(512)}, /*index=5*/f32[384]{0:T(512)}, ...) fusion(f32[2,1182,384]{2,1,0:T(8,128)} %copy-done, ...), kind=kLoop, calls=%fused_computation.169 | loop fusion | flops 38921472 | bytes 74362368 | tf_op jit(solution)/shard_map/reduce_sum | solution.py:104
  194.3 1.3 collective-permute-start.2
  195.6 3.7 collective-permute-start.3
  199.3 7.0 %fusion.106 = bf16[1536,384]{0,1:T(8,128)(2,1)} fusion(bf16[2,1152,384]{2,1,0:T(8,128)(2,1)S(1)} %copy-done.64, bf16[2,1152,1536]{2,1,0:T(8,128)(2,1)} %param.19), kind=kOutput, calls=%fused_computation.216 | convolution fusion | flops 2718498816 | bytes 10027008 | tf_op jit(solution)/shard_map/dot_general | solution.py:23
  206.3 2.4 copy.47
  208.9 33.2 %multiply_bitcast_fusion.1 = (bf16[2,1152,1,384]{3,1,0,2:T(8,128)(2,1)S(1)}, f32[2,1152,384]{2,1,0:T(8,128)S(1)}) fusion(f32[2,1152,2,384]{3,1,2,0:T(8,128)} %copy-done.3, f32[2,1152]{1,0:T(2,128)S(1)} %compare_convert_fusion, f32[384]{0:T(512)} %get-tuple-element.94, f32[2,1152,384]{2,1,0:T(8,128)S(1)} %get-tuple-element.102, ...), kind=kLoop, calls=%fused_computation.201 | loop fusion | flops 85819392 | bytes 12535296 | tf_op jit(solution)/shard_map/stack | solution.py:116
  242.2 4.2 multiply_bitcast_fusion
  246.8 34.2 %copy.33 = bf16[2,1152,2,384]{3,2,1,0:T(2,128)(2,1)S(1)} copy(bf16[2,1152,2,384]{3,1,0,2:T(8,128)(2,1)S(1)} %maximum_convert_fusion) | data formatting | bytes 7077888 | tf_op jit(solution)/shard_map/convert_element_type | solution.py:117
  281.0 2.4 copy.51
  283.4 5.8 %copy.34 = bf16[768,2304]{1,0:T(8,128)(2,1)} copy(bf16[768,2304]{0,1:T(8,128)(2,1)} %bitcast.81) | data formatting | bytes 7077888 | tf_op jit(solution)/shard_map/dot_general | solution.py:23
  289.3 10.0 %convolution_convert_fusion.2 = bf16[1536,2,384]{2,0,1:T(8,128)(2,1)} fusion(bf16[2304,1536,1]{1,0,2:T(8,128)(2,1)} %bitcast.86, bf16[2,384,2304]{2,1,0:T(8,128)(2,1)} %bitcast.87), kind=kOutput, calls=%fused_computation.212 | convolution fusion | flops 5436997632 | bytes 12976128 | tf_op jit(solution)/shard_map/dot_general | solution.py:23
  299.4 8.5 %convolution_convert_fusion.1 = bf16[2304,1536]{1,0:T(8,128)(2,1)} fusion(bf16[2304,384]{1,0:T(8,128)(2,1)} %bitcast.95, bf16[1536,384]{1,0:T(8,128)(2,1)} %all-gather.5.cloned.1.call-done), kind=kOutput, calls=%fused_computation.32 | convolution fusion | flops 2721447936 | bytes 10027008 | tf_op jit(solution)/shard_map/dot_general | solution.py:23
  307.9 10.2 %copy.43 = bf16[2304,1536]{0,1:T(8,128)(2,1)} copy(bf16[2304,1536]{1,0:T(8,128)(2,1)} %convolution_convert_fusion.1) | data formatting | bytes 14155776
  318.3 10.3 %convolution_convert_fusion = bf16[2304,1536]{1,0:T(8,128)(2,1)} fusion(bf16[2304,768]{1,0:T(8,128)(2,1)} %bitcast.82, bf16[1536,768]{1,0:T(8,128)(2,1)} %bitcast.85), kind=kOutput, calls=%fused_computation.31 | convolution fusion | flops 5439356928 | bytes 12976128 | tf_op jit(solution)/shard_map/dot_general | solution.py:23
  328.6 9.9 %copy.45 = bf16[2304,1536]{0,1:T(8,128)(2,1)} copy(bf16[2304,1536]{1,0:T(8,128)(2,1)} %convolution_convert_fusion) | data formatting | bytes 14155776
  340.6 10.9 %bitcast_convert_fusion = f32[2304,1536]{1,0:T(8,128)} fusion(bf16[2,1152,1536]{2,1,0:T(8,128)(2,1)} %param.10), kind=kLoop, calls=%fused_computation.264 | loop fusion | flops 3538944 | bytes 21233664 | tf_op jit(solution)/shard_map/reshape | solution.py:76
  351.7 6.0 %multiply_reduce_fusion.2 = (f32[384]{0:T(512)S(1)}, f32[384]{0:T(512)S(1)}, f32[384]{0:T(512)S(1)}, f32[384]{0:T(512)S(1)}, f32[384]{0:T(512)S(1)}, /*index=5*/...) fusion(f32[2,1152,384]{2,1,0:T(8,128)S(1)} %get-tuple-element.1, ...), kind=kLoop, calls=%fused_computation.170 | loop fusion | flops 22998144 | bytes 49565184 | tf_op jit(solution)/shard_map/reduce_sum | solution.py:104
  360.8 2.1 copy.37
  363.0 50.2 %reduce-scatter.13.cloned.1.call-done = bf16[384,2304]{1,0:T(8,128)(2,1)} async-done(((bf16[1536,2304]{1,0:T(8,128)(2,1)}), bf16[384,2304]{1,0:T(8,128)(2,1)}) %reduce-scatter.13.cloned.1.call-update) | async-done | bytes 1769488
  413.2 2.8 copy.44
  415.9 3.6 add_convert_fusion.1
  419.5 73.1 %reduce-scatter.15.cloned.1.call-done = bf16[384,2304]{1,0:T(8,128)(2,1)} async-done(((bf16[1536,2304]{1,0:T(8,128)(2,1)}), bf16[384,2304]{1,0:T(8,128)(2,1)}) %reduce-scatter.15.cloned.1.call-update) | async-done | bytes 1769488
  492.7 2.8 copy.46
  495.4 3.2 fusion.11
  498.7 29.4 %all-reduce = (f32[31,384]{1,0:T(8,128)}, f32[2,384]{1,0:T(2,128)}) all-reduce(f32[31,384]{1,0:T(8,128)S(1)} %stack.157, f32[2,384]{1,0:T(2,128)S(1)} %pad_maximum_fusion.3), channel_id=1, replica_groups=mesh['ctx'=8,'chan'=4] {'ctx'}, use_global_device_ids=true, to_apply=%region_50.0 | all-reduce | flops 12672 | bytes 101376 | tf_op jit(solution)/shard_map/psum | solution.py:152
  528.2 15.4 %all-reduce.2 = (f32[2304]{0:T(1024)S(1)}, f32[2304]{0:T(1024)S(1)}) all-reduce(f32[2304]{0:T(1024)S(1)} %get-tuple-element.29, f32[2304]{0:T(1024)S(1)} %get-tuple-element.63), channel_id=1, replica_groups=mesh['ctx'=8,'chan'=4] {'chan'}, use_global_device_ids=true, to_apply=%region_16.0 | all-reduce | flops 4608 | bytes 36864 | tf_op jit(solution)/shard_map/psum | solution.py:139
  543.6 4.5 fusion.9
  (201 shorter events, 14.3 us)
Async XLA Ops:
  7.2 36.6 %all-gather.3.cloned.1.call-start = ((), (), s32[]{:S(2)}) async-start(), calls=%async_computation.4 | async-start | bytes 2654208 | tf_op jit(solution)/shard_map/all_gather | solution.py:48
  7.9 121.2 %all-gather.5.cloned.1.call-start = ((), (), s32[]{:S(2)}) async-start(), calls=%async_computation.5 | async-start | bytes 1327104 | tf_op jit(solution)/shard_map/all_gather | solution.py:72
  8.6 350.3 %reduce-scatter.17.cloned.1.call-start = ((), (), s32[]{:S(2)}) async-start(), calls=%async_computation.9 | async-start | bytes 1327104
  12.2 5.0 copy-start.2
  17.2 2.0 copy-start.63
  17.3 2.1 copy-start.41
  17.3 2.1 copy-start.42
  19.3 10.9 %copy-start.7 = (f32[2,1152]{1,0:T(2,128)}, f32[2,1152]{1,0:T(2,128)S(1)}, u32[]{:S(2)}) copy-start(f32[2,1152]{1,0:T(2,128)S(1)} %add_rsqrt_fusion) | copy-start | bytes 27652
  45.9 11.6 %copy-start.5 = (bf16[192,8,2,384]{3,1,2,0:T(8,128)(2,1)}, bf16[192,8,2,384]{3,1,2,0:T(8,128)(2,1)S(1)}, u32[]{:S(2)}) copy-start(bf16[192,8,2,384]{3,1,2,0:T(8,128)(2,1)S(1)} %copy.50) | copy-start | bytes 7077892
  57.5 2.9 copy-start.3
  60.4 1.2 copy-start.6
  61.7 4.0 collective-permute-start
  63.8 3.8 collective-permute-start.1
  76.5 0.7 copy-start.29
  76.5 0.7 copy-start.30
  76.6 0.7 copy-start.35
  76.6 0.7 copy-start.40
  76.9 15.7 %copy-start = (f32[2,1182,384]{2,1,0:T(8,128)}, f32[2,1182,384]{2,1,0:T(8,128)S(1)}, u32[]{:S(2)}) copy-start(f32[2,1182,384]{2,1,0:T(8,128)S(1)} %convert_element_type.79) | copy-start | bytes 10893316
  92.6 46.8 %copy-start.4 = (f32[2,1152,384]{2,1,0:T(8,128)}, f32[2,1152,384]{2,1,0:T(8,128)S(1)}, u32[]{:S(2)}) copy-start(f32[2,1152,384]{2,1,0:T(8,128)S(1)} %get-tuple-element.108) | copy-start | bytes 10616836
  153.7 45.6 %copy-start.64 = (bf16[2,1152,384]{2,1,0:T(8,128)(2,1)S(1)}, bf16[2,1152,384]{2,1,0:T(8,128)(2,1)}, u32[]{:S(2)}) copy-start(bf16[2,1152,384]{2,1,0:T(8,128)(2,1)} %get-tuple-element.111) | copy-start | bytes 5308420
  194.3 14.6 %collective-permute-start.2 = (f32[2,15,384]{2,1,0:T(8,128)}, f32[2,15,384]{2,1,0:T(8,128)}, u32[]{:S(2)}, u32[]{:S(2)}) collective-permute-start(f32[2,15,384]{2,1,0:T(8,128)} %get-tuple-element.112), channel_id=1, source_target_pairs={{4,0},{8,4},{12,8},{16,12},{20,16},{24,20},{28,24},{5,1},{9,5},{13... | collective-permute-start | bytes 138248 | tf_op jit(solution)/shard_map/ppermute | solution.py:17
  195.6 13.3 %collective-permute-start.3 = (f32[2,15,384]{2,1,0:T(8,128)}, f32[2,15,384]{2,1,0:T(8,128)}, u32[]{:S(2)}, u32[]{:S(2)}) collective-permute-start(f32[2,15,384]{2,1,0:T(8,128)} %get-tuple-element.113), channel_id=1, source_target_pairs={{0,4},{4,8},{8,12},{12,16},{16,20},{20,24},{24,28},{1,5},{5,9},{9,... | collective-permute-start | bytes 138248 | tf_op jit(solution)/shard_map/ppermute | solution.py:16
  208.7 152.1 %reduce-scatter.11.cloned.1.call-start = ((), (), s32[]{:S(2)}) async-start(), calls=%async_computation.6 | async-start | bytes 2654208 | tf_op jit(solution)/shard_map/reduce_scatter | solution.py:121
  299.3 113.9 %reduce-scatter.13.cloned.1.call-start = ((), (), s32[]{:S(2)}) async-start(), calls=%async_computation.7 | async-start | bytes 8847360
  318.1 174.6 %reduce-scatter.15.cloned.1.call-start = ((), (), s32[]{:S(2)}) async-start(), calls=%async_computation.8 | async-start | bytes 8847360
  338.5 0.7 copy-start.8
  340.6 10.9 %copy-start.62 = (f32[384]{0:T(512)S(1)}, f32[384]{0:T(512)}, u32[]{:S(2)}) copy-start(f32[384]{0:T(512)} %get-tuple-element.98) | copy-start | bytes 4612
  340.6 10.9 %copy-start.61 = (f32[384]{0:T(512)S(1)}, f32[384]{0:T(512)}, u32[]{:S(2)}) copy-start(f32[384]{0:T(512)} %get-tuple-element.99) | copy-start | bytes 4612
  340.6 10.9 %copy-start.1 = (f32[2,1182,384]{2,1,0:T(8,128)S(1)}, f32[2,1182,384]{2,1,0:T(8,128)}, u32[]{:S(2)}) copy-start(f32[2,1182,384]{2,1,0:T(8,128)} %copy-done) | copy-start | bytes 10893316
  351.5 6.3 %copy-start.60 = (f32[384]{0:T(512)S(1)}, f32[384]{0:T(512)}, u32[]{:S(2)}) copy-start(f32[384]{0:T(512)} %get-tuple-element.47) | copy-start | bytes 4612
  351.5 6.3 %copy-start.59 = (f32[384]{0:T(512)S(1)}, f32[384]{0:T(512)}, u32[]{:S(2)}) copy-start(f32[384]{0:T(512)} %get-tuple-element.46) | copy-start | bytes 4612
  351.5 6.4 %copy-start.58 = (f32[384]{0:T(512)S(1)}, f32[384]{0:T(512)}, u32[]{:S(2)}) copy-start(f32[384]{0:T(512)} %get-tuple-element.45) | copy-start | bytes 4612
  351.5 6.4 %copy-start.57 = (f32[384]{0:T(512)S(1)}, f32[384]{0:T(512)}, u32[]{:S(2)}) copy-start(f32[384]{0:T(512)} %get-tuple-element.44) | copy-start | bytes 4612
  351.5 6.4 %copy-start.56 = (f32[384]{0:T(512)S(1)}, f32[384]{0:T(512)}, u32[]{:S(2)}) copy-start(f32[384]{0:T(512)} %get-tuple-element.43) | copy-start | bytes 4612
  351.6 6.4 %copy-start.55 = (f32[384]{0:T(512)S(1)}, f32[384]{0:T(512)}, u32[]{:S(2)}) copy-start(f32[384]{0:T(512)} %get-tuple-element.42) | copy-start | bytes 4612
  351.6 6.4 %copy-start.54 = (f32[384]{0:T(512)S(1)}, f32[384]{0:T(512)}, u32[]{:S(2)}) copy-start(f32[384]{0:T(512)} %get-tuple-element.41) | copy-start | bytes 4612
  351.6 6.4 %copy-start.53 = (f32[384]{0:T(512)S(1)}, f32[384]{0:T(512)}, u32[]{:S(2)}) copy-start(f32[384]{0:T(512)} %get-tuple-element.40) | copy-start | bytes 4612
  351.6 6.4 %copy-start.52 = (f32[384]{0:T(512)S(1)}, f32[384]{0:T(512)}, u32[]{:S(2)}) copy-start(f32[384]{0:T(512)} %get-tuple-element.39) | copy-start | bytes 4612
  351.6 6.4 %copy-start.51 = (f32[384]{0:T(512)S(1)}, f32[384]{0:T(512)}, u32[]{:S(2)}) copy-start(f32[384]{0:T(512)} %get-tuple-element.38) | copy-start | bytes 4612
  351.6 6.4 %copy-start.50 = (f32[384]{0:T(512)S(1)}, f32[384]{0:T(512)}, u32[]{:S(2)}) copy-start(f32[384]{0:T(512)} %get-tuple-element.37) | copy-start | bytes 4612
  351.6 6.5 %copy-start.49 = (f32[384]{0:T(512)S(1)}, f32[384]{0:T(512)}, u32[]{:S(2)}) copy-start(f32[384]{0:T(512)} %get-tuple-element.36) | copy-start | bytes 4612
  351.6 6.5 %copy-start.48 = (f32[384]{0:T(512)S(1)}, f32[384]{0:T(512)}, u32[]{:S(2)}) copy-start(f32[384]{0:T(512)} %get-tuple-element.35) | copy-start | bytes 4612
  351.6 6.5 %copy-start.47 = (f32[384]{0:T(512)S(1)}, f32[384]{0:T(512)}, u32[]{:S(2)}) copy-start(f32[384]{0:T(512)} %get-tuple-element.34) | copy-start | bytes 4612
  351.6 6.5 %copy-start.46 = (f32[384]{0:T(512)S(1)}, f32[384]{0:T(512)}, u32[]{:S(2)}) copy-start(f32[384]{0:T(512)} %get-tuple-element.33) | copy-start | bytes 4612
  351.7 6.5 %copy-start.45 = (f32[384]{0:T(512)S(1)}, f32[384]{0:T(512)}, u32[]{:S(2)}) copy-start(f32[384]{0:T(512)} %get-tuple-element.32) | copy-start | bytes 4612
  351.7 6.5 %copy-start.44 = (f32[384]{0:T(512)S(1)}, f32[384]{0:T(512)}, u32[]{:S(2)}) copy-start(f32[384]{0:T(512)} %get-tuple-element.31) | copy-start | bytes 4612
  351.7 6.5 %copy-start.43 = (f32[384]{0:T(512)S(1)}, f32[384]{0:T(512)}, u32[]{:S(2)}) copy-start(f32[384]{0:T(512)} %get-tuple-element.30) | copy-start | bytes 4612
  495.4 48.2 %copy-start.9 = (f32[2304]{0:T(1024)S(1)}, f32[2304]{0:T(1024)}, u32[]{:S(2)}) copy-start(f32[2304]{0:T(1024)} %rsqrt.20) | copy-start | bytes 27652
  (27 other events, 18.1 us)
Sparse Core Ops, SparseCore 0:
  9.6 34.1 all-gather.2
  45.4 22.0 all-gather.4
  208.8 31.2 reduce-scatter.16
  299.4 35.3 reduce-scatter.10
  337.8 75.3 reduce-scatter.12
  416.1 76.5 reduce-scatter.14
where the time goes:
time: 565 us; the launch traced here: 555 us
  other arithmetic  145 us (26%)
  waiting for transfers between devices  140 us (25%)
  local copies, waits for them, and re-layouts  99.7 us (18%)
  blocking collectives  90.7 us (16%)
  matrix products  54.8 us (10%)
  between operations  15.4 us (3%)
  starting transfers between devices  8.95 us (2%)
    unnamed x9, waiting for transfers between devices  125 us
    reduce_sum x2, other arithmetic, on_device(): jnp.sum(grad_depth * padded[:, offset:offset + local_len], axis=(0, 1))  46 us
    unnamed x140, local copies, waits for them, and re-layouts  42.2 us
    another operation x2, other arithmetic, on_device(): jnp.stack([grad_values, grad_gates], axis=2).astype(jnp.bfloat16)  37.4 us
    dot_general x4, matrix products, contract(): lax.dot_general(left_op, right_op, (((left_dim,), (right_dim,)), ((), ())...  35.8 us
    convert_element_type x1, local copies, waits for them, and re-layouts, on_device(): grad_proj = jnp.stack([grad_values, grad_gates], axis=2).astype(jnp.bfloa...  34.2 us
    psum x1, blocking collectives, on_device(): grad_w_depth, grad_ln = lax.psum((depth_local, ln_local), 'ctx')  29.4 us
    psum x1, blocking collectives, on_device(): lax.psum(jnp.sum(depth_out * valid_mask, axis=(0, 1)), 'ctx') / frame_count  16.8 us
  transfers between devices with their start and end apart: 10, of which 4 were waited for; matrix products, arithmetic and copies ran while one was open for 42% of the time, Pallas kernels for 0%

commit v1 on v0

--- a/solution.py
+++ b/solution.py
@@ -60,7 +60,10 @@
     depth_out = jnp.zeros((records, local_len, channels), jnp.float32)
     for offset in range(tap_count):
         depth_out = depth_out + padded[:, offset : offset + local_len] * w_depth[offset]
-    bn_mean = lax.psum(jnp.sum(depth_out * valid_mask, axis=(0, 1)), "ctx") / frame_count
+    bn_mean = (
+        lax.all_gather(jnp.sum(depth_out * valid_mask, axis=(0, 1)), "ctx").sum(axis=0)
+        / frame_count
+    )
     bn_cent = (depth_out - bn_mean) * valid_mask
     bn_var = lax.psum(jnp.sum(bn_cent * bn_cent, axis=(0, 1)), "ctx") / frame_count
     bn_rstd = lax.rsqrt(bn_var + epsilon)

time: 565 us -> 564 us (level)
    psum x1 -> x0, blocking collectives: 16.8 us -> none  [on_device(): lax.psum(jnp.sum(depth_out * valid_mask, axis=(0, 1)), 'ctx') / frame_count]
    all_gather x0 -> x1, blocking collectives: none -> 14.1 us  [on_device(): lax.all_gather(jnp.sum(depth_out * valid_mask, axis=(0, 1)), 'ctx')]
    unnamed x140 -> x141, local copies, waits for them, and re-layouts: 42.2 us -> 42.2 us
where the time goes in v1:
time: 564 us; the launch traced here: 554 us
  other arithmetic  146 us (26%)
  waiting for transfers between devices  140 us (25%)
  local copies, waits for them, and re-layouts  99.7 us (18%)
  blocking collectives  88.7 us (16%)
  matrix products  54.9 us (10%)
  between operations  15.6 us (3%)
  starting transfers between devices  8.95 us (2%)
    unnamed x9, waiting for transfers between devices  125 us
    reduce_sum x2, other arithmetic, on_device(): jnp.sum(grad_depth * padded[:, offset:offset + local_len], axis=(0, 1))  46 us
    unnamed x141, local copies, waits for them, and re-layouts  42.2 us
    another operation x2, other arithmetic, on_device(): jnp.stack([grad_values, grad_gates], axis=2).astype(jnp.bfloat16)  37.4 us
    dot_general x4, matrix products, contract(): lax.dot_general(left_op, right_op, (((left_dim,), (right_dim,)), ((), ())...  35.8 us
    convert_element_type x1, local copies, waits for them, and re-layouts, on_device(): grad_proj = jnp.stack([grad_values, grad_gates], axis=2).astype(jnp.bfloa...  34.2 us
    psum x1, blocking collectives, on_device(): grad_w_depth, grad_ln = lax.psum((depth_local, ln_local), 'ctx')  29.4 us
    psum x1, blocking collectives, on_device(): lax.psum(jnp.sum(bn_cent * bn_cent, axis=(0, 1)), 'ctx') / frame_count  15.5 us
  transfers between devices with their start and end apart: 10, of which 4 were waited for; matrix products, arithmetic and copies ran while one was open for 42% of the time, Pallas kernels for 0%

profile of v1, /device:TPU:0, one launch (start us, length us, event | category | flops | bytes accessed | tf_op | source)
XLA Modules:
  0.0 554.2 jit_solution(5017218447660173859)
XLA Ops:
  8.7 1.9 slice_reduce_fusion.30
  10.6 1.7 slice_reduce_fusion.29
  12.2 4.2 convert_reduce_fusion
  17.3 2.0 multiply_reduce_fusion
  19.4 10.8 %subtract_multiply_fusion = (f32[2,1152,1536]{2,1,0:T(8,128)}, bf16[2,1152,1536]{2,1,0:T(8,128)(2,1)}) fusion(bf16[2,1152,1536]{2,1,0:T(8,128)(2,1)} %param.10, f32[2,1152]{1,0:T(2,128)S(1)} %add_rsqrt_fusion, f32[2,1152]{1,0:T(2,128)S(1)} %broadcast_multiply_fusion.2, f32[1536]{0:T(1024)S(1)} %copy-done.42, f32[1536]{0:T(1024)S(1)} %copy-done.41), kind=kLoop, calls=%fused_computation.30 | loop fusion | flops 21233664 | bytes 28342272 | tf_op jit(solution)/shard_map/mul | solution.py:45
  30.2 13.6 %all-gather.5.cloned.1.call-done = bf16[1536,2,384]{2,1,0:T(2,128)(2,1)} async-done(((bf16[192,2,384]{2,1,0:T(2,128)(2,1)}), bf16[1536,2,384]{2,1,0:T(2,128)(2,1)}) %all-gather.5.cloned.1.call-update) | async-done | bytes 2359312 | tf_op jit(solution)/shard_map/all_gather | solution.py:48
  43.8 2.1 copy.50
  45.9 2.8 copy.31
  48.8 8.7 %fusion = f32[2,1152,2,384]{3,1,2,0:T(8,128)S(1)} fusion(bf16[2,384,1536,1]{2,1,0,3:T(8,128)(2,1)} %bitcast.89, bf16[2,1152,1536]{2,1,0:T(8,128)(2,1)} %get-tuple-element.110), kind=kOutput, calls=%fused_computation.35 | convolution fusion | flops 5435817984 | bytes 16515072 | tf_op jit(solution)/shard_map/dot_general | solution.py:50
  58.7 1.8 copy-done.3
  61.7 2.1 collective-permute-start
  63.8 1.3 collective-permute-start.1
  65.7 1.9 collective-permute-done.1
  67.5 8.8 %concatenate.38 = bf16[2,1182,384]{2,1,0:T(8,128)(2,1)S(1)} concatenate(bf16[2,15,384]{2,1,0:T(8,128)(2,1)S(1)} %collective-permute-done, bf16[2,1152,384]{2,1,0:T(8,128)(2,1)} %copy-done.6, bf16[2,15,384]{2,1,0:T(8,128)(2,1)S(1)} %collective-permute-done.1), dimensions={1} | concatenate | bytes 3631104 | tf_op jit(solution)/shard_map/concatenate | solution.py:18
  77.3 14.7 %multiply_reduce_fusion.34 = (f32[384]{0:T(512)S(1)}, f32[2,1152,384]{2,1,0:T(8,128)S(1)}) fusion(f32[2,1152]{1,0:T(2,128)S(1)} %compare_convert_fusion, f32[384]{0:T(512)S(1)} %copy-done.39, f32[2,1182,384]{2,1,0:T(8,128)S(1)} %convert_element_type.79, f32[384]{0:T(512)S(1)} %copy-done.40, f32[384]{0:T(512)S(1)} %copy-done.10, f32[384]{0:T(512)S(1)} %copy-done.11, ...), kind=kLoop, calls=%fused_computation.209 | loop fusion | flops 55737984 | bytes 113304576 | tf_op jit(solution)/shard_map/reduce_sum | solution.py:64
  92.1 14.1 %all-gather.1 = f32[8,1,384]{2,1,0:T(1,128)} all-gather(f32[1,1,384]{2,1,0:T(1,128)S(1)} %reshape.178), channel_id=2, replica_groups=mesh['ctx'=8,'chan'=4] {'ctx'}, dimensions={0}, use_global_device_ids=true | all-gather | bytes 13824 | tf_op jit(solution)/shard_map/all_gather | solution.py:64
  106.2 1.3 reduce_sum.390
  107.5 1.3 broadcast_divide_fusion
  110.5 15.5 %psum.49 = f32[384]{0:T(512)} all-reduce(f32[384]{0:T(512)} %multiply_reduce_fusion.33), channel_id=1, replica_groups=mesh['ctx'=8,'chan'=4] {'ctx'}, use_global_device_ids=true, to_apply=%region_6.0 | all-reduce | flops 384 | bytes 3072 | tf_op jit(solution)/shard_map/psum | solution.py:68
  125.9 1.9 fusion.110
  127.9 10.3 %fusion.108 = (f32[384]{0:T(512)}, f32[384]{0:T(512)}, bf16[2,1152,384]{2,1,0:T(8,128)(2,1)}, f32[2,1152,384]{2,1,0:T(8,128)}) fusion(f32[384]{0:T(512)} %get-tuple-element.106, f32[2,1152,384]{2,1,0:T(8,128)S(1)} %get-tuple-element.108, f32[384]{0:T(512)} %copy-done.28, f32[2,1152]{1,0:T(2,128)S(1)} %compare_convert_fusion, f32[384]{0:T(512)} %param.16, ...), kind=kOutput, calls=%fused_computation.260 | convolution fusion | flops 2734717952 | bytes 17123328 | tf_op jit(solution)/shard_map/dot_general | solution.py:91
  138.2 14.3 %all-reduce.1 = (f32[384]{0:T(512)}, f32[384]{0:T(512)}) all-reduce(f32[384]{0:T(512)} %get-tuple-element.62, f32[384]{0:T(512)} %get-tuple-element.61), channel_id=1, replica_groups=mesh['ctx'=8,'chan'=4] {'ctx'}, use_global_device_ids=true, to_apply=%region_11.0 | all-reduce | flops 768 | bytes 6144 | tf_op jit(solution)/shard_map/psum | solution.py:96
  152.5 40.0 %multiply_reduce_fusion.1 = (f32[384]{0:T(512)}, f32[384]{0:T(512)}, f32[384]{0:T(512)}, f32[384]{0:T(512)}, f32[384]{0:T(512)}, /*index=5*/f32[384]{0:T(512)}, ...) fusion(f32[2,1182,384]{2,1,0:T(8,128)} %copy-done, ...), kind=kLoop, calls=%fused_computation.169 | loop fusion | flops 38921472 | bytes 74362368 | tf_op jit(solution)/shard_map/reduce_sum | solution.py:107
  194.4 3.7 collective-permute-start.3
  198.0 7.0 %fusion.106 = bf16[1536,384]{0,1:T(8,128)(2,1)} fusion(bf16[2,1152,384]{2,1,0:T(8,128)(2,1)S(1)} %copy-done.64, bf16[2,1152,1536]{2,1,0:T(8,128)(2,1)} %param.19), kind=kOutput, calls=%fused_computation.216 | convolution fusion | flops 2718498816 | bytes 10027008 | tf_op jit(solution)/shard_map/dot_general | solution.py:23
  205.0 2.4 copy.47
  207.7 33.2 %multiply_bitcast_fusion.1 = (bf16[2,1152,1,384]{3,1,0,2:T(8,128)(2,1)S(1)}, f32[2,1152,384]{2,1,0:T(8,128)S(1)}) fusion(f32[2,1152,2,384]{3,1,2,0:T(8,128)} %copy-done.3, f32[2,1152]{1,0:T(2,128)S(1)} %compare_convert_fusion, f32[384]{0:T(512)} %get-tuple-element.94, f32[2,1152,384]{2,1,0:T(8,128)S(1)} %get-tuple-element.102, ...), kind=kLoop, calls=%fused_computation.201 | loop fusion | flops 85819392 | bytes 12535296 | tf_op jit(solution)/shard_map/stack | solution.py:119
  240.9 4.2 multiply_bitcast_fusion
  245.6 34.2 %copy.33 = bf16[2,1152,2,384]{3,2,1,0:T(2,128)(2,1)S(1)} copy(bf16[2,1152,2,384]{3,1,0,2:T(8,128)(2,1)S(1)} %maximum_convert_fusion) | data formatting | bytes 7077888 | tf_op jit(solution)/shard_map/convert_element_type | solution.py:120
  279.8 2.4 copy.51
  282.2 5.8 %copy.34 = bf16[768,2304]{1,0:T(8,128)(2,1)} copy(bf16[768,2304]{0,1:T(8,128)(2,1)} %bitcast.81) | data formatting | bytes 7077888 | tf_op jit(solution)/shard_map/dot_general | solution.py:23
  288.0 10.0 %convolution_convert_fusion.2 = bf16[1536,2,384]{2,0,1:T(8,128)(2,1)} fusion(bf16[2304,1536,1]{1,0,2:T(8,128)(2,1)} %bitcast.86, bf16[2,384,2304]{2,1,0:T(8,128)(2,1)} %bitcast.87), kind=kOutput, calls=%fused_computation.212 | convolution fusion | flops 5436997632 | bytes 12976128 | tf_op jit(solution)/shard_map/dot_general | solution.py:23
  298.1 8.5 %convolution_convert_fusion.1 = bf16[2304,1536]{1,0:T(8,128)(2,1)} fusion(bf16[2304,384]{1,0:T(8,128)(2,1)} %bitcast.95, bf16[1536,384]{1,0:T(8,128)(2,1)} %all-gather.7.cloned.1.call-done), kind=kOutput, calls=%fused_computation.32 | convolution fusion | flops 2721447936 | bytes 10027008 | tf_op jit(solution)/shard_map/dot_general | solution.py:23
  306.6 10.2 %copy.43 = bf16[2304,1536]{0,1:T(8,128)(2,1)} copy(bf16[2304,1536]{1,0:T(8,128)(2,1)} %convolution_convert_fusion.1) | data formatting | bytes 14155776
  317.1 10.3 %convolution_convert_fusion = bf16[2304,1536]{1,0:T(8,128)(2,1)} fusion(bf16[2304,768]{1,0:T(8,128)(2,1)} %bitcast.82, bf16[1536,768]{1,0:T(8,128)(2,1)} %bitcast.85), kind=kOutput, calls=%fused_computation.31 | convolution fusion | flops 5439356928 | bytes 12976128 | tf_op jit(solution)/shard_map/dot_general | solution.py:23
  327.4 9.9 %copy.45 = bf16[2304,1536]{0,1:T(8,128)(2,1)} copy(bf16[2304,1536]{1,0:T(8,128)(2,1)} %convolution_convert_fusion) | data formatting | bytes 14155776
  339.3 10.8 %bitcast_convert_fusion = f32[2304,1536]{1,0:T(8,128)} fusion(bf16[2,1152,1536]{2,1,0:T(8,128)(2,1)} %param.10), kind=kLoop, calls=%fused_computation.264 | loop fusion | flops 3538944 | bytes 21233664 | tf_op jit(solution)/shard_map/reshape | solution.py:79
  350.4 6.0 %multiply_reduce_fusion.2 = (f32[384]{0:T(512)S(1)}, f32[384]{0:T(512)S(1)}, f32[384]{0:T(512)S(1)}, f32[384]{0:T(512)S(1)}, f32[384]{0:T(512)S(1)}, /*index=5*/...) fusion(f32[2,1152,384]{2,1,0:T(8,128)S(1)} %get-tuple-element.1, ...), kind=kLoop, calls=%fused_computation.170 | loop fusion | flops 22998144 | bytes 49565184 | tf_op jit(solution)/shard_map/reduce_sum | solution.py:107
  359.5 2.1 copy.37
  361.6 50.4 %reduce-scatter.13.cloned.1.call-done = bf16[384,2304]{1,0:T(8,128)(2,1)} async-done(((bf16[1536,2304]{1,0:T(8,128)(2,1)}), bf16[384,2304]{1,0:T(8,128)(2,1)}) %reduce-scatter.13.cloned.1.call-update) | async-done | bytes 1769488
  412.0 2.8 copy.44
  414.8 3.6 add_convert_fusion.1
  418.4 73.2 %reduce-scatter.15.cloned.1.call-done = bf16[384,2304]{1,0:T(8,128)(2,1)} async-done(((bf16[1536,2304]{1,0:T(8,128)(2,1)}), bf16[384,2304]{1,0:T(8,128)(2,1)}) %reduce-scatter.15.cloned.1.call-update) | async-done | bytes 1769488
  491.5 2.8 copy.46
  494.3 3.2 fusion.11
  497.6 29.4 %all-reduce = (f32[31,384]{1,0:T(8,128)}, f32[2,384]{1,0:T(2,128)}) all-reduce(f32[31,384]{1,0:T(8,128)S(1)} %stack.157, f32[2,384]{1,0:T(2,128)S(1)} %pad_maximum_fusion.3), channel_id=1, replica_groups=mesh['ctx'=8,'chan'=4] {'ctx'}, use_global_device_ids=true, to_apply=%region_50.0 | all-reduce | flops 12672 | bytes 101376 | tf_op jit(solution)/shard_map/psum | solution.py:155
  527.0 15.4 %all-reduce.2 = (f32[2304]{0:T(1024)S(1)}, f32[2304]{0:T(1024)S(1)}) all-reduce(f32[2304]{0:T(1024)S(1)} %get-tuple-element.29, f32[2304]{0:T(1024)S(1)} %get-tuple-element.63), channel_id=1, replica_groups=mesh['ctx'=8,'chan'=4] {'chan'}, use_global_device_ids=true, to_apply=%region_16.0 | all-reduce | flops 4608 | bytes 36864 | tf_op jit(solution)/shard_map/psum | solution.py:142
  542.5 4.5 fusion.9
  (203 shorter events, 15.6 us)
Async XLA Ops:
  7.2 36.6 %all-gather.5.cloned.1.call-start = ((), (), s32[]{:S(2)}) async-start(), calls=%async_computation.4 | async-start | bytes 2654208 | tf_op jit(solution)/shard_map/all_gather | solution.py:48
  7.9 120.0 %all-gather.7.cloned.1.call-start = ((), (), s32[]{:S(2)}) async-start(), calls=%async_computation.5 | async-start | bytes 1327104 | tf_op jit(solution)/shard_map/all_gather | solution.py:75
  8.6 349.0 %reduce-scatter.17.cloned.1.call-start = ((), (), s32[]{:S(2)}) async-start(), calls=%async_computation.9 | async-start | bytes 1327104
  12.2 5.0 copy-start.2
  17.2 2.0 copy-start.63
  17.3 2.1 copy-start.41
  17.3 2.1 copy-start.42
  19.3 10.9 %copy-start.7 = (f32[2,1152]{1,0:T(2,128)}, f32[2,1152]{1,0:T(2,128)S(1)}, u32[]{:S(2)}) copy-start(f32[2,1152]{1,0:T(2,128)S(1)} %add_rsqrt_fusion) | copy-start | bytes 27652
  45.9 11.6 %copy-start.5 = (bf16[192,8,2,384]{3,1,2,0:T(8,128)(2,1)}, bf16[192,8,2,384]{3,1,2,0:T(8,128)(2,1)S(1)}, u32[]{:S(2)}) copy-start(bf16[192,8,2,384]{3,1,2,0:T(8,128)(2,1)S(1)} %copy.50) | copy-start | bytes 7077892
  57.5 2.9 copy-start.3
  60.4 1.2 copy-start.6
  61.7 4.0 collective-permute-start
  63.8 3.8 collective-permute-start.1
  76.5 0.7 copy-start.29
  76.5 0.7 copy-start.30
  76.6 0.7 copy-start.35
  76.6 0.7 copy-start.40
  76.9 15.1 %copy-start = (f32[2,1182,384]{2,1,0:T(8,128)}, f32[2,1182,384]{2,1,0:T(8,128)S(1)}, u32[]{:S(2)}) copy-start(f32[2,1182,384]{2,1,0:T(8,128)S(1)} %convert_element_type.79) | copy-start | bytes 10893316
  92.0 46.1 %copy-start.4 = (f32[2,1152,384]{2,1,0:T(8,128)}, f32[2,1152,384]{2,1,0:T(8,128)S(1)}, u32[]{:S(2)}) copy-start(f32[2,1152,384]{2,1,0:T(8,128)S(1)} %get-tuple-element.108) | copy-start | bytes 10616836
  152.5 45.6 %copy-start.64 = (bf16[2,1152,384]{2,1,0:T(8,128)(2,1)S(1)}, bf16[2,1152,384]{2,1,0:T(8,128)(2,1)}, u32[]{:S(2)}) copy-start(bf16[2,1152,384]{2,1,0:T(8,128)(2,1)} %get-tuple-element.111) | copy-start | bytes 5308420
  193.1 14.6 %collective-permute-start.2 = (f32[2,15,384]{2,1,0:T(8,128)}, f32[2,15,384]{2,1,0:T(8,128)}, u32[]{:S(2)}, u32[]{:S(2)}) collective-permute-start(f32[2,15,384]{2,1,0:T(8,128)} %get-tuple-element.112), channel_id=1, source_target_pairs={{4,0},{8,4},{12,8},{16,12},{20,16},{24,20},{28,24},{5,1},{9,5},{13... | collective-permute-start | bytes 138248 | tf_op jit(solution)/shard_map/ppermute | solution.py:17
  194.4 13.3 %collective-permute-start.3 = (f32[2,15,384]{2,1,0:T(8,128)}, f32[2,15,384]{2,1,0:T(8,128)}, u32[]{:S(2)}, u32[]{:S(2)}) collective-permute-start(f32[2,15,384]{2,1,0:T(8,128)} %get-tuple-element.113), channel_id=1, source_target_pairs={{0,4},{4,8},{8,12},{12,16},{16,20},{20,24},{24,28},{1,5},{5,9},{9,... | collective-permute-start | bytes 138248 | tf_op jit(solution)/shard_map/ppermute | solution.py:16
  207.5 152.1 %reduce-scatter.11.cloned.1.call-start = ((), (), s32[]{:S(2)}) async-start(), calls=%async_computation.6 | async-start | bytes 2654208 | tf_op jit(solution)/shard_map/reduce_scatter | solution.py:124
  298.1 113.9 %reduce-scatter.13.cloned.1.call-start = ((), (), s32[]{:S(2)}) async-start(), calls=%async_computation.7 | async-start | bytes 8847360
  316.8 174.7 %reduce-scatter.15.cloned.1.call-start = ((), (), s32[]{:S(2)}) async-start(), calls=%async_computation.8 | async-start | bytes 8847360
  337.3 0.7 copy-start.8
  339.3 10.8 %copy-start.62 = (f32[384]{0:T(512)S(1)}, f32[384]{0:T(512)}, u32[]{:S(2)}) copy-start(f32[384]{0:T(512)} %get-tuple-element.98) | copy-start | bytes 4612
  339.3 10.8 %copy-start.61 = (f32[384]{0:T(512)S(1)}, f32[384]{0:T(512)}, u32[]{:S(2)}) copy-start(f32[384]{0:T(512)} %get-tuple-element.99) | copy-start | bytes 4612
  339.3 10.8 %copy-start.1 = (f32[2,1182,384]{2,1,0:T(8,128)S(1)}, f32[2,1182,384]{2,1,0:T(8,128)}, u32[]{:S(2)}) copy-start(f32[2,1182,384]{2,1,0:T(8,128)} %copy-done) | copy-start | bytes 10893316
  350.2 6.3 %copy-start.60 = (f32[384]{0:T(512)S(1)}, f32[384]{0:T(512)}, u32[]{:S(2)}) copy-start(f32[384]{0:T(512)} %get-tuple-element.47) | copy-start | bytes 4612
  350.2 6.3 %copy-start.59 = (f32[384]{0:T(512)S(1)}, f32[384]{0:T(512)}, u32[]{:S(2)}) copy-start(f32[384]{0:T(512)} %get-tuple-element.46) | copy-start | bytes 4612
  350.2 6.4 %copy-start.58 = (f32[384]{0:T(512)S(1)}, f32[384]{0:T(512)}, u32[]{:S(2)}) copy-start(f32[384]{0:T(512)} %get-tuple-element.45) | copy-start | bytes 4612
  350.2 6.4 %copy-start.57 = (f32[384]{0:T(512)S(1)}, f32[384]{0:T(512)}, u32[]{:S(2)}) copy-start(f32[384]{0:T(512)} %get-tuple-element.44) | copy-start | bytes 4612
  350.2 6.4 %copy-start.56 = (f32[384]{0:T(512)S(1)}, f32[384]{0:T(512)}, u32[]{:S(2)}) copy-start(f32[384]{0:T(512)} %get-tuple-element.43) | copy-start | bytes 4612
  350.3 6.4 %copy-start.55 = (f32[384]{0:T(512)S(1)}, f32[384]{0:T(512)}, u32[]{:S(2)}) copy-start(f32[384]{0:T(512)} %get-tuple-element.42) | copy-start | bytes 4612
  350.3 6.4 %copy-start.54 = (f32[384]{0:T(512)S(1)}, f32[384]{0:T(512)}, u32[]{:S(2)}) copy-start(f32[384]{0:T(512)} %get-tuple-element.41) | copy-start | bytes 4612
  350.3 6.4 %copy-start.53 = (f32[384]{0:T(512)S(1)}, f32[384]{0:T(512)}, u32[]{:S(2)}) copy-start(f32[384]{0:T(512)} %get-tuple-element.40) | copy-start | bytes 4612
  350.3 6.4 %copy-start.52 = (f32[384]{0:T(512)S(1)}, f32[384]{0:T(512)}, u32[]{:S(2)}) copy-start(f32[384]{0:T(512)} %get-tuple-element.39) | copy-start | bytes 4612
  350.3 6.4 %copy-start.51 = (f32[384]{0:T(512)S(1)}, f32[384]{0:T(512)}, u32[]{:S(2)}) copy-start(f32[384]{0:T(512)} %get-tuple-element.38) | copy-start | bytes 4612
  350.3 6.4 %copy-start.50 = (f32[384]{0:T(512)S(1)}, f32[384]{0:T(512)}, u32[]{:S(2)}) copy-start(f32[384]{0:T(512)} %get-tuple-element.37) | copy-start | bytes 4612
  350.3 6.5 %copy-start.49 = (f32[384]{0:T(512)S(1)}, f32[384]{0:T(512)}, u32[]{:S(2)}) copy-start(f32[384]{0:T(512)} %get-tuple-element.36) | copy-start | bytes 4612
  350.3 6.5 %copy-start.48 = (f32[384]{0:T(512)S(1)}, f32[384]{0:T(512)}, u32[]{:S(2)}) copy-start(f32[384]{0:T(512)} %get-tuple-element.35) | copy-start | bytes 4612
  350.3 6.5 %copy-start.47 = (f32[384]{0:T(512)S(1)}, f32[384]{0:T(512)}, u32[]{:S(2)}) copy-start(f32[384]{0:T(512)} %get-tuple-element.34) | copy-start | bytes 4612
  350.3 6.5 %copy-start.46 = (f32[384]{0:T(512)S(1)}, f32[384]{0:T(512)}, u32[]{:S(2)}) copy-start(f32[384]{0:T(512)} %get-tuple-element.33) | copy-start | bytes 4612
  350.4 6.5 %copy-start.45 = (f32[384]{0:T(512)S(1)}, f32[384]{0:T(512)}, u32[]{:S(2)}) copy-start(f32[384]{0:T(512)} %get-tuple-element.32) | copy-start | bytes 4612
  350.4 6.5 %copy-start.44 = (f32[384]{0:T(512)S(1)}, f32[384]{0:T(512)}, u32[]{:S(2)}) copy-start(f32[384]{0:T(512)} %get-tuple-element.31) | copy-start | bytes 4612
  350.4 6.5 %copy-start.43 = (f32[384]{0:T(512)S(1)}, f32[384]{0:T(512)}, u32[]{:S(2)}) copy-start(f32[384]{0:T(512)} %get-tuple-element.30) | copy-start | bytes 4612
  494.3 48.2 %copy-start.9 = (f32[2304]{0:T(1024)S(1)}, f32[2304]{0:T(1024)}, u32[]{:S(2)}) copy-start(f32[2304]{0:T(1024)} %rsqrt.20) | copy-start | bytes 27652
  (27 other events, 18.1 us)
Sparse Core Ops, SparseCore 0:
  9.6 34.1 all-gather.4
  45.4 22.0 all-gather.6
  207.6 31.3 reduce-scatter.16
  298.2 35.4 reduce-scatter.10
  336.6 75.3 reduce-scatter.12
  414.9 76.5 reduce-scatter.14
